TPU v7x, 128 devices: a whole 4x4x4 slice. The times are simulated.
128 devices in a mesh: freq: 8 (over x, y_lo), tm: 16 (over z, y_hi, core).
Axes of the slice: x: 4, y: 4 (y_hi: 2, y_lo: 2; y = y_hi * 2 + y_lo), z: 4, core: 2. Of those that a mesh axis runs over, the one named last changes fastest.
Arguments:
- voltages: bfloat16 [2048, 530432], P(('tm', 'freq')), may hold values from -128 to 127, as said below
- fir_taps: float32 [4, 2048], replicated, may hold values from -3 to 3
Outputs:
- coherence: bfloat16 [2, 64, 2048, 2048], P(None, 'freq', 'tm')
Inputs may be any that keep to these rules, and one draw needn't show every extreme that they name: `voltages`: every sample is a whole number.
All inputs are finite; a program needn't handle non-finite values.
Results may differ from a plain program's by a relative error of at most 0.0073.
Values may be sent and summed in bfloat16 or wider, within the bound.
A program may use at most 192 MiB of HBM per device.

v0:
```python
import math

import jax
import jax.numpy as jnp
from jax import lax
from jax.sharding import PartitionSpec as P

P_SIZE = 2048
TAPS = 4
FIRST_BIN = 512
CH_DEV = 8
S = 256


def dft_table(channels):
    points = jnp.arange(P_SIZE, dtype=jnp.int32)
    bins = FIRST_BIN + jnp.arange(channels, dtype=jnp.int32)
    phase = points[:, None] * bins[None, :] % P_SIZE
    angle = 2.0 * math.pi / P_SIZE * phase.astype(jnp.float32)
    twiddle = jnp.stack([jnp.cos(angle), -jnp.sin(angle)], axis=2)
    return twiddle.reshape(P_SIZE, 2 * channels).astype(jnp.bfloat16)


def filter_frames(block, fir_taps):
    inputs_here = block.shape[0]
    samples = block.astype(jnp.float32).reshape(inputs_here, S + TAPS - 1, P_SIZE)
    frames = fir_taps[0] * samples[:, 0:S]
    for tap_index in range(1, TAPS):
        frames = frames + fir_taps[tap_index] * samples[:, tap_index : tap_index + S]
    return frames.astype(jnp.bfloat16).reshape(inputs_here * S, P_SIZE)


def correlate(own_spectra, column_block):
    slab = own_spectra.shape[0]
    rows_here = own_spectra.shape[2]
    width = column_block.shape[2]
    left_rows = own_spectra.reshape(slab, 2 * rows_here, S)
    right_rows = column_block.reshape(slab, 2 * width, S)
    products = lax.dot_general(
        left_rows, right_rows, (((2,), (2,)), ((0,), (0,))), preferred_element_type=jnp.float32
    )
    products = products.reshape(slab, 2, rows_here, 2, width)
    real_part = products[:, 0, :, 0] + products[:, 1, :, 1]
    imag_part = products[:, 1, :, 0] - products[:, 0, :, 1]
    return jnp.stack([real_part, imag_part])


def on_device(voltages, fir_taps):
    freq_count = lax.axis_size("freq")
    channels = CH_DEV * freq_count
    inputs_here = voltages.shape[0]
    frames = filter_frames(voltages, fir_taps)
    twiddle = dft_table(channels)
    spectra = lax.dot_general(
        twiddle, frames, (((0,), (1,)), ((), ())), preferred_element_type=jnp.float32
    )
    spectra = spectra.astype(jnp.bfloat16).reshape(channels, 2, inputs_here, S)
    own_spectra = lax.all_to_all(spectra, "freq", split_axis=0, concat_axis=2, tiled=True)
    all_spectra = lax.all_gather(own_spectra, "tm", axis=2, tiled=True)
    raw_sums = correlate(own_spectra, all_spectra)
    wide = own_spectra.astype(jnp.float32)
    powers = jnp.sum(wide * wide, axis=(1, 3)) / S + 1e-06
    powers_all = lax.all_gather(powers, "tm", axis=1, tiled=True)
    row_scale = lax.rsqrt(powers) / S
    column_scale = lax.rsqrt(powers_all)
    coherence = raw_sums * row_scale[None, :, :, None] * column_scale[None, :, None, :]
    return coherence.astype(jnp.bfloat16)


def solution(mesh):
    placed = (P(("tm", "freq"), None), P())
    return jax.shard_map(
        on_device,
        mesh=mesh,
        in_specs=placed,
        out_specs=P(None, "freq", "tm", None),
        check_vma=False,
    )
```

profile of v0, /device:TPU:0, one launch (start us, length us, event | category | flops | bytes accessed | tf_op | source)
XLA Modules:
  0.0 372.8 jit_solution(2463869961442593070)
XLA Ops:
  6.5 0.0 all-gather.2.cloned.1.call-start
  6.5 0.9 fusion.15
  7.5 2.5 cosine_convert_fusion
  9.9 0.1 pad_maximum_fusion
  10.0 0.5 copy.13
  10.5 0.2 convert_element_type.41
  10.8 25.4 %reshape.197 = f32[16,259,2048]{2,1,0:T(8,128)} reshape(bf16[16,530432]{1,0:T(8,128)(2,1)} %param.2) | data formatting | bytes 50921472 | tf_op jit(solution)/shard_map/reshape | solution.py:26
  36.1 49.4 %fusion.1 = bf16[16,256,2048]{2,1,0:T(8,128)(2,1)} fusion(f32[16,259,2048]{2,1,0:T(8,128)} %reshape.197, f32[2048]{0:T(1024)S(1)} %bitcast.36, f32[2048]{0:T(1024)S(1)} %bitcast.37, f32[2048]{0:T(1024)S(1)} %bitcast.35, f32[2048]{0:T(1024)S(1)} %bitcast.34), kind=kLoop, calls=%fused_computation.2 | loop fusion | flops 67108864 | bytes 151027712 | tf_op jit(solution)/shard_map/convert_element_type | solution.py:30
  85.5 11.4 %convolution_convert_fusion = bf16[128,4096]{1,0:T(8,128)(2,1)S(1)} fusion(bf16[2048,128]{0,1:T(8,128)(2,1)S(1)} %convert_element_type.41, bf16[4096,2048]{1,0:T(8,128)(2,1)} %bitcast.26), kind=kOutput, calls=%fused_computation.15 | convolution fusion | flops 2148007936 | bytes 18350080 | tf_op jit(solution)/shard_map/dot_general | solution.py:54
  96.9 0.2 copy.23
  97.2 20.5 %all_to_all.18 = bf16[64,2,16,256]{3,2,1,0:T(8,128)(2,1)S(1)} all-to-all(bf16[64,2,16,256]{3,2,1,0:T(8,128)(2,1)S(1)} %bitcast.33), channel_id=1, replica_groups=mesh['freq'=8,'tm'=16] {'freq'}, dimensions={0} | all-to-all | bytes 2097152 | tf_op jit(solution)/shard_map/all_to_all | solution.py:58
  117.7 1.1 copy.14
  118.8 0.0 all-gather.2.cloned.1.call-update
  118.8 0.3 multiply_reduce_fusion
  119.1 0.1 add.76
  119.2 26.1 %all_gather.7 = f32[8,2048]{1,0:T(8,128)S(1)} all-gather(f32[8,128]{1,0:T(8,128)S(1)} %add.76), channel_id=1, replica_groups=mesh['freq'=8,'tm'=16] {'tm'}, dimensions={1}, use_global_device_ids=true | all-gather | bytes 69632 | tf_op jit(solution)/shard_map/all_gather | solution.py:63
  145.3 84.0 %all-gather.2.cloned.1.call-done = bf16[8,2,2048,256]{3,2,1,0:T(8,128)(2,1)} async-done(((bf16[8,2,128,256]{3,2,1,0:T(8,128)(2,1)}), bf16[8,2,2048,256]{3,2,1,0:T(8,128)(2,1)}) %all-gather.2.cloned.1.call-update) | async-done | bytes 16777232 | tf_op jit(solution)/shard_map/all_gather | solution.py:59
  229.3 17.4 %fusion.16 = f32[8,256,4096]{2,1,0:T(8,128)} fusion(bf16[8,256,256]{2,1,0:T(8,128)(2,1)} %bitcast.29, bf16[8,4096,256]{2,1,0:T(8,128)(2,1)} %bitcast.27), kind=kOutput, calls=%fused_computation.34 | convolution fusion | flops 4294967296 | bytes 51380224 | tf_op jit(solution)/shard_map/dot_general | solution.py:39
  246.8 42.6 %reshape.195 = f32[8,2,128,2,2048]{4,3,2,1,0:T(2,128)} reshape(f32[8,256,4096]{2,1,0:T(8,128)} %fusion.16) | data formatting | bytes 67108864 | tf_op jit(solution)/shard_map/reshape | solution.py:42
  289.4 39.8 %fusion.14 = (f32[8,1,128,1,2048]{4,3,2,1,0:T(1,128)}, f32[8,1,128,1,2048]{4,3,2,1,0:T(1,128)}, f32[8,1,128,1,2048]{4,3,2,1,0:T(1,128)}, f32[8,1,128,1,2048]{4,3,2,1,0:T(1,128)}) fusion(f32[8,2,128,2,2048]{4,3,2,1,0:T(2,128)} %reshape.195), kind=kLoop, calls=%fused_computation.32 | loop fusion | bytes 67108864 | tf_op jit(solution)/shard_map/slice | solution.py:43
  329.2 26.8 %fusion.6 = (f32[1,8,128,2048]{3,2,1,0:T(8,128)}, f32[1,8,128,2048]{3,2,1,0:T(8,128)}) fusion(f32[8,1,128,1,2048]{4,3,2,1,0:T(1,128)} %get-tuple-element.8, f32[8,1,128,1,2048]{4,3,2,1,0:T(1,128)} %get-tuple-element.6, f32[8,1,128,1,2048]{4,3,2,1,0:T(1,128)} %get-tuple-element.7, f32[8,1,128,1,2048]{4,3,2,1,0:T(1,128)} %get-tuple-element.5), kind=kLoop, calls=%fused_computation.12 | loop fusion | flops 4194304 | bytes 50331648 | tf_op jit(solution)/shard_map/sub | solution.py:44
  356.0 9.9 %fusion.5 = bf16[2,8,128,2048]{3,2,1,0:T(8,128)(2,1)} fusion(f32[1,8,128,2048]{3,2,1,0:T(8,128)} %get-tuple-element.15, f32[1,8,128,2048]{3,2,1,0:T(8,128)} %get-tuple-element.16, f32[8,2048]{1,0:T(8,128)S(1)} %rsqrt.11, f32[8,128]{1,0:T(8,128)S(1)} %rsqrt_multiply_fusion), kind=kLoop, calls=%fused_computation.10 | loop fusion | flops 16777216 | bytes 25235456 | tf_op jit(solution)/shard_map/convert_element_type | solution.py:67
  (4 shorter events, 0.0 us)
Async XLA Ops:
  6.5 222.8 %all-gather.2.cloned.1.call-start = ((), (), s32[]{:S(2)}) async-start(), calls=%async_computation.1 | async-start | bytes 17825792 | tf_op jit(solution)/shard_map/all_gather | solution.py:59
Sparse Core Ops, SparseCore 0:
  118.9 110.3 all-gather.1
where the time goes:
time: 375 us; the launch traced here: 373 us
  local copies, waits for them, and re-layouts  111 us (30%)
  other arithmetic  88.9 us (24%)
  waiting for transfers between devices  84 us (22%)
  blocking collectives  46.6 us (12%)
  matrix products  28.8 us (8%)
  between operations  13.5 us (4%)
    all_gather x1, waiting for transfers between devices, on_device(): all_spectra = lax.all_gather(own_spectra, 'tm', axis=2, tiled=True)  84 us
    convert_element_type x1, other arithmetic, filter_frames(): return frames.astype(jnp.bfloat16).reshape(inputs_here * S, P_SIZE)  49.4 us
    reshape x1, local copies, waits for them, and re-layouts, correlate(): products = products.reshape(slab, 2, rows_here, 2, width)  42.6 us
    slice x1, local copies, waits for them, and re-layouts, correlate(): real_part = products[:, 0, :, 0] + products[:, 1, :, 1]  39.8 us
    sub x1, other arithmetic, correlate(): imag_part = products[:, 1, :, 0] - products[:, 0, :, 1]  26.8 us
    all_gather x1, blocking collectives, on_device(): powers_all = lax.all_gather(powers, 'tm', axis=1, tiled=True)  26.1 us
    reshape x1, local copies, waits for them, and re-layouts, filter_frames(): block.astype(jnp.float32).reshape(inputs_here, S + TAPS - 1, P_SIZE)  25.4 us
    all_to_all x1, blocking collectives, on_device(): lax.all_to_all(spectra, 'freq', split_axis=0, concat_axis=2, tiled=True)  20.5 us
  transfers between devices with their start and end apart: 1, of which 1 were waited for; matrix products, arithmetic and copies ran while one was open for 0% of the time, Pallas kernels for 0%

commit v1 on v0

v1 whole, which is shorter than its diff:
```python
import functools

import jax
import jax.numpy as jnp
import ml_dtypes
import numpy as np
from jax import lax
from jax.experimental import pallas as pl
from jax.experimental.pallas import tpu as pltpu
from jax.sharding import PartitionSpec as P

P_SIZE = 2048
TAPS = 4
FIRST_BIN = 512
CH_DEV = 8
S = 256
A_DEV = 16
CHANNELS = 64
S_BLOCK = 32
ROWS = 128
TM = 16
FREQ = 8
MESH = pl.DeviceIdType.MESH
MIB = 1 << 20


def dft_table():
    points = np.arange(P_SIZE, dtype=np.int64)
    bins = FIRST_BIN + np.arange(CHANNELS, dtype=np.int64)
    angle = 2.0 * np.pi / P_SIZE * (points[:, None] * bins[None, :] % P_SIZE)
    table = np.concatenate([np.cos(angle), -np.sin(angle)], axis=1)
    return table.astype(ml_dtypes.bfloat16)


def channelize_kernel(v_hbm, taps_ref, table_ref, out_ref, v, frames, raw, turned, sem):
    blocks = S // S_BLOCK

    def load(i):
        low = 0 if i == 0 else (i * S_BLOCK + TAPS - 1) * P_SIZE
        high = ((i + 1) * S_BLOCK + TAPS - 1) * P_SIZE
        return pltpu.make_async_copy(v_hbm.at[:, low:high], v.at[:, low:high], sem.at[i])

    for i in range(blocks):
        load(i).start()
    for i in range(blocks):
        load(i).wait()

        def filter_columns(chunk, _, i=i):
            column = pl.multiple_of(chunk * 128, 128)
            taps = [
                jnp.broadcast_to(taps_ref[k : k + 1, pl.ds(column, 128)], (A_DEV, 128))
                for k in range(TAPS)
            ]

            def sample(s):
                return v[:, pl.ds(s * P_SIZE + column, 128)].astype(jnp.float32)

            first = i * S_BLOCK
            window = [sample(first + k) for k in range(TAPS - 1)]
            for s in range(S_BLOCK):
                window.append(sample(first + s + TAPS - 1))
                total = taps[0] * window[0]
                for k in range(1, TAPS):
                    total = total + taps[k] * window[k]
                frames[s * A_DEV : (s + 1) * A_DEV, pl.ds(column, 128)] = total.astype(jnp.bfloat16)
                window = window[1:]
            return 0

        lax.fori_loop(0, P_SIZE // 128, filter_columns, 0)
        raw[i * S_BLOCK * A_DEV : (i + 1) * S_BLOCK * A_DEV, :] = jnp.dot(
            frames[...], table_ref[...], preferred_element_type=jnp.float32
        )

    def turn(a, _):
        spectra = raw[pl.ds(a, S, A_DEV), :].T
        re, im = spectra[:CHANNELS], spectra[CHANNELS:]
        power = jnp.sum(re * re + im * im, axis=1, keepdims=True) / S + 1e-6
        scale = lax.rsqrt(power) * (1.0 / 16.0)
        for h in range(2):
            lanes = slice(h * 128, (h + 1) * 128)
            turned[h, pl.ds(a, CHANNELS, 2 * A_DEV), :] = (re * scale)[:, lanes]
            turned[h, pl.ds(a + A_DEV, CHANNELS, 2 * A_DEV), :] = (im * scale)[:, lanes]
        return 0

    lax.fori_loop(0, A_DEV, turn, 0)
    for h in range(2):
        out_ref[:, h * 128 : (h + 1) * 128] = turned[h].astype(jnp.bfloat16)


def channelize(voltages, fir_taps):
    rows = 2 * CHANNELS * A_DEV
    return pl.pallas_call(
        channelize_kernel,
        out_shape=jax.ShapeDtypeStruct((rows, S), jnp.bfloat16),
        in_specs=[
            pl.BlockSpec(memory_space=pl.ANY),
            pl.BlockSpec(memory_space=pltpu.VMEM),
            pl.BlockSpec(memory_space=pltpu.VMEM),
        ],
        out_specs=pl.BlockSpec(memory_space=pltpu.VMEM),
        scratch_shapes=[
            pltpu.VMEM((A_DEV, (S + TAPS - 1) * P_SIZE), jnp.bfloat16),
            pltpu.VMEM((S_BLOCK * A_DEV, P_SIZE), jnp.bfloat16),
            pltpu.VMEM((S * A_DEV, 128), jnp.float32),
            pltpu.VMEM((2, rows, 128), jnp.float32),
            pltpu.SemaphoreType.DMA((S // S_BLOCK,)),
        ],
        compiler_params=pltpu.CompilerParams(vmem_limit_bytes=56 * MIB),
        name="channelize",
    )(voltages, fir_taps, jnp.asarray(dft_table()))


def correlate_kernel(
    spectra, out_ref, held, a2a_send, a2a_recv, y_send, y_recv, z_send, z_recv, f_send, f_recv, c_send, c_recv
):
    f = lax.axis_index("freq")
    t = lax.axis_index("tm")
    z, yh, core = t // 4, t // 2 % 2, t % 2

    def owner(dz, other_y, other_core=0):
        return (z + dz) % 4 * 4 + (yh + other_y) % 2 * 2 + (core + other_core) % 2

    def there(dz, other_y, other_core=0):
        return {"freq": f, "tm": owner(dz, other_y, other_core)}

    up, down, across, sibling = there(1, 0), there(3, 0), there(0, 1), there(0, 0, 1)
    peers = [{"freq": (f + j) % FREQ, "tm": t} for j in range(1, FREQ)]

    barrier = pltpu.get_barrier_semaphore()
    greeted = [up, down, across, sibling, *peers]
    for device in greeted:
        pl.semaphore_signal(barrier, inc=1, device_id=device, device_id_type=MESH)
    pl.semaphore_wait(barrier, len(greeted))

    started = []

    def send(src, dst, send_sem, recv_sem, device):
        copy = pltpu.make_async_remote_copy(
            src_ref=src,
            dst_ref=dst,
            send_sem=send_sem,
            recv_sem=recv_sem,
            device_id=device,
            device_id_type=MESH,
        )
        copy.start()
        started.append((src, send_sem))

    def arrived(ref, sem):
        pltpu.make_async_copy(ref, ref, sem).wait()

    def share(c, slot, dz, other_y):
        block = held.at[c, owner(dz, other_y)]
        send(block, block, c_send.at[c, slot], c_recv.at[c, slot], sibling)

    def whole_up_down(c, plane):
        block = held.at[c, owner(0, plane)]
        send(block, block, z_send.at[c, plane, 0], z_recv.at[c, plane, 0], up)
        send(block, block, z_send.at[c, plane, 1], z_recv.at[c, plane, 1], down)

    def forward(c, plane):
        low, high = held.at[c, owner(3, plane)], held.at[c, owner(1, plane)]
        arrived(low, z_recv.at[c, plane, 0])
        send(low.at[0], low.at[0], f_send.at[c, plane, 0], f_recv.at[c, plane, 0], up)
        arrived(high, z_recv.at[c, plane, 1])
        send(high.at[1], high.at[1], f_send.at[c, plane, 1], f_recv.at[c, plane, 1], down)

    slab_rows = pl.ds(pl.multiple_of(f * A_DEV, A_DEV), A_DEV)
    for c in range(CH_DEV):
        mine = held.at[c, t, :, slab_rows]
        for j, device in enumerate(peers):
            send(spectra.at[device["freq"], c], mine, a2a_send.at[c, j], a2a_recv.at[c], device)
        pltpu.make_async_copy(spectra.at[f, c], mine, a2a_recv.at[c]).start()

    def stage_own(c):
        block = held.at[c, t]
        arrived(block, a2a_recv.at[c])
        send(block, block, y_send.at[c], y_recv.at[c], across)
        whole_up_down(c, 0)
        share(c, 0, 0, 0)

    def stage_across(c):
        arrived(held.at[c, owner(0, 1)], y_recv.at[c])
        whole_up_down(c, 1)
        share(c, 1, 0, 1)

    def stage_forward(c, plane):
        forward(c, plane)
        share(c, 2 + plane, 3, plane)
        share(c, 4 + plane, 1, plane)

    def stage_far(c):
        for plane in range(2):
            far = held.at[c, owner(2, plane)]
            arrived(far.at[0], f_recv.at[c, plane, 0])
            arrived(far.at[1], f_recv.at[c, plane, 1])
            share(c, 6 + plane, 2, plane)

    def stage_correlate(c):
        for slot, (dz, plane) in enumerate([(0, 0), (0, 1), (3, 0), (3, 1), (1, 0), (1, 1), (2, 0), (2, 1)]):
            arrived(held.at[c, owner(dz, plane, 1)], c_recv.at[c, slot])
        rows = held[c, t].reshape(2 * ROWS, S)

        def column_block(b, _):
            columns = held[c, b].reshape(2 * ROWS, S)
            products = lax.dot_general(
                rows, columns, (((1,), (1,)), ((), ())), preferred_element_type=jnp.float32
            )
            lanes = pl.ds(pl.multiple_of(b * ROWS, ROWS), ROWS)
            re = products[:ROWS, :ROWS] + products[ROWS:, ROWS:]
            im = products[ROWS:, :ROWS] - products[:ROWS, ROWS:]
            out_ref[0, c, :, lanes] = re.astype(jnp.bfloat16)
            out_ref[1, c, :, lanes] = im.astype(jnp.bfloat16)
            return 0

        lax.fori_loop(0, TM, column_block, 0)

    stages = [
        (0, stage_own),
        (1, stage_across),
        (1, functools.partial(stage_forward, plane=0)),
        (2, functools.partial(stage_forward, plane=1)),
        (3, stage_far),
        (4, stage_correlate),
    ]
    for step in range(CH_DEV + 4):
        for lag, stage in stages:
            if 0 <= step - lag < CH_DEV:
                stage(step - lag)
    for src, sem in started:
        arrived(src, sem)


def correlate(spectra):
    dma = pltpu.SemaphoreType.DMA
    return pl.pallas_call(
        correlate_kernel,
        out_shape=jax.ShapeDtypeStruct((2, CH_DEV, ROWS, TM * ROWS), jnp.bfloat16),
        in_specs=[pl.BlockSpec(memory_space=pltpu.VMEM)],
        out_specs=pl.BlockSpec(memory_space=pltpu.VMEM),
        scratch_shapes=[
            pltpu.VMEM((CH_DEV, TM, 2, ROWS, S), jnp.bfloat16),
            dma((CH_DEV, FREQ - 1)),
            dma((CH_DEV,)),
            dma((CH_DEV,)),
            dma((CH_DEV,)),
            dma((CH_DEV, 2, 2)),
            dma((CH_DEV, 2, 2)),
            dma((CH_DEV, 2, 2)),
            dma((CH_DEV, 2, 2)),
            dma((CH_DEV, 8)),
            dma((CH_DEV, 8)),
        ],
        compiler_params=pltpu.CompilerParams(
            collective_id=0, has_side_effects=True, vmem_limit_bytes=40 * MIB
        ),
        name="gather_correlate",
    )(spectra)


def on_device(voltages, fir_taps):
    spectra = channelize(voltages, fir_taps)
    return correlate(spectra.reshape(FREQ, CH_DEV, 2, A_DEV, S))


def solution(mesh):
    placed = (P(("tm", "freq"), None), P())
    return jax.shard_map(
        on_device,
        mesh=mesh,
        in_specs=placed,
        out_specs=P(None, "freq", "tm", None),
        check_vma=False,
    )
```

time: 375 us -> 144 us (0.38)
  Pallas kernels: 0 us -> 130 us
  local copies, waits for them, and re-layouts: 111 us -> 12.9 us
  other arithmetic: 88.9 us -> 0 us
  waiting for transfers between devices: 84 us -> 0 us
  blocking collectives: 46.6 us -> 0 us
  matrix products: 28.8 us -> 0 us
  between operations: 13.5 us -> 0.03 us
    pallas_call x0 -> x2, Pallas kernels: none -> 130 us  [the longest x1 101 us: correlate(): pl.pallas_call(correlate_kernel, out_shape=jax.ShapeDtypeStruct((2, CH_DE...]
    all_gather x1 -> x0, waiting for transfers between devices: 84 us -> none  [on_device(): all_spectra = lax.all_gather(own_spectra, 'tm', axis=2, tiled=True)]
    reshape x2 -> x0, local copies, waits for them, and re-layouts: 68 us -> none  [the longest x1 42.6 us: correlate(): products = products.reshape(slab, 2, rows_here, 2, width)]
    convert_element_type x2 -> x0, other arithmetic: 59.3 us -> none  [the longest x1 49.4 us: filter_frames(): return frames.astype(jnp.bfloat16).reshape(inputs_here * S, P_SIZE)]
    slice x2 -> x0, local copies, waits for them, and re-layouts: 40.8 us -> none  [the longest x1 39.8 us: correlate(): real_part = products[:, 0, :, 0] + products[:, 1, :, 1]]
    dot_general x2 -> x0, matrix products: 28.8 us -> none  [the longest x1 17.4 us: correlate(): lax.dot_general(left_rows, right_rows, (((2,), (2,)), ((0,), (0,))), pref...]
    sub x1 -> x0, other arithmetic: 26.8 us -> none  [correlate(): imag_part = products[:, 1, :, 0] - products[:, 0, :, 1]]
    all_gather x1 -> x0, blocking collectives: 26.1 us -> none  [on_device(): powers_all = lax.all_gather(powers, 'tm', axis=1, tiled=True)]
  transfers between devices with their start and end apart: 1 -> 0, of which waited for: 1 -> 0; matrix products, arithmetic and copies ran while one was open for 0% -> 0% of each run, Pallas kernels for 0% -> 0%
where the time goes in v1:
time: 144 us; the launch traced here: 143 us
  Pallas kernels  130 us (90%)
  local copies, waits for them, and re-layouts  12.9 us (9%)
    pallas_call x1, Pallas kernels, correlate(): pl.pallas_call(correlate_kernel, out_shape=jax.ShapeDtypeStruct((2, CH_DE...  101 us
    pallas_call x1, Pallas kernels, channelize(): pl.pallas_call(channelize_kernel, out_shape=jax.ShapeDtypeStruct((rows, S...  29.5 us
    unnamed x5, local copies, waits for them, and re-layouts  12.9 us

profile of v1, /device:TPU:0, one launch (start us, length us, event | category | flops | bytes accessed | tf_op | source)
XLA Modules:
  0.0 143.4 jit_solution(10149790251236889928)
XLA Ops:
  0.0 29.5 %channelize.1 = bf16[2048,256]{1,0:T(8,128)(2,1)} custom-call(bf16[16,530432]{1,0:T(8,128)(2,1)} %v_hbm.1, f32[4,2048]{1,0:T(4,128)} %taps_ref.1, bf16[2048,128]{1,0:T(8,128)(2,1)} %constant.2.clone.table_ref), custom_call_target="tpu_custom_call" | custom-call | tf_op jit(solution)/shard_map/channelize/pallas_call | solution.py:92
  29.5 0.0 copy-start.1
  29.5 1.2 copy-done.1
  30.7 101.0 %gather_correlate.1 = bf16[2,8,128,2048]{3,2,1,0:T(8,128)(2,1)S(1)} custom-call(bf16[8,8,2,16,256]{4,3,2,1,0:T(8,128)(2,1)S(1)} %bitcast.1), custom_call_target="tpu_custom_call" | custom-call | tf_op jit(solution)/shard_map/gather_correlate/pallas_call | solution.py:236
  131.7 0.0 copy-start
  131.7 3.2 %copy-done = bf16[2,8,128,2048]{3,2,1,0:T(8,128)(2,1)} copy-done((bf16[2,8,128,2048]{3,2,1,0:T(8,128)(2,1)}, bf16[2,8,128,2048]{3,2,1,0:T(8,128)(2,1)S(1)}, u32[]{:S(2)}) %copy-start) | copy-done | bytes 8388632
  134.9 8.4 %copy.5 = bf16[2,8,128,2048]{3,2,1,0:T(8,128)(2,1)} copy(bf16[2,8,128,2048]{3,2,1,0:T(8,128)(2,1)} %copy-done) | data formatting | bytes 16777216
Async XLA Ops:
  29.5 1.2 copy-start.1
  131.7 3.2 %copy-start = (bf16[2,8,128,2048]{3,2,1,0:T(8,128)(2,1)}, bf16[2,8,128,2048]{3,2,1,0:T(8,128)(2,1)S(1)}, u32[]{:S(2)}) copy-start(bf16[2,8,128,2048]{3,2,1,0:T(8,128)(2,1)S(1)} %gather_correlate.1) | copy-start | bytes 25165828

commit v2 on v1

--- a/solution.py
+++ b/solution.py
@@ -22,6 +22,10 @@
 FREQ = 8
 MESH = pl.DeviceIdType.MESH
 MIB = 1 << 20
+Z_FIRST = (0, 2, 4)
+OWN_PACE = 0.5
+Y_TIMES = {"own": 0.0, "near": 2.0, "across": 2.0, "near_across": 4.0, "far": 5.5, "correlate": 6.5}
+Z_TIMES = {"own": 0.0, "near": 1.5, "fan": 1.5, "far": 3.0, "across": 6.0, "correlate": 7.0}
 
 
 def dft_table():
@@ -111,7 +115,7 @@
 
 
 def correlate_kernel(
-    spectra, out_ref, held, a2a_send, a2a_recv, y_send, y_recv, z_send, z_recv, f_send, f_recv, c_send, c_recv
+    spectra, out_ref, held, a2a_send, a2a_recv, b_send, y_send, y_recv, z_send, z_recv, f_send, f_recv, c_send, c_recv
 ):
     f = lax.axis_index("freq")
     t = lax.axis_index("tm")
@@ -124,10 +128,12 @@
         return {"freq": f, "tm": owner(dz, other_y, other_core)}
 
     up, down, across, sibling = there(1, 0), there(3, 0), there(0, 1), there(0, 0, 1)
+    x, yl = f // 2, f % 2
     peers = [{"freq": (f + j) % FREQ, "tm": t} for j in range(1, FREQ)]
+    beyond = [{"freq": (x + j) % 4 * 2 + 1 - yl, "tm": owner(0, 1)} for j in range(4)]
 
     barrier = pltpu.get_barrier_semaphore()
-    greeted = [up, down, across, sibling, *peers]
+    greeted = [up, down, across, sibling, *peers, *beyond]
     for device in greeted:
         pl.semaphore_signal(barrier, inc=1, device_id=device, device_id_type=MESH)
     pl.semaphore_wait(barrier, len(greeted))
@@ -165,36 +171,54 @@
         arrived(high, z_recv.at[c, plane, 1])
         send(high.at[1], high.at[1], f_send.at[c, plane, 1], f_recv.at[c, plane, 1], down)
 
-    slab_rows = pl.ds(pl.multiple_of(f * A_DEV, A_DEV), A_DEV)
     for c in range(CH_DEV):
-        mine = held.at[c, t, :, slab_rows]
+        mine = held.at[c, t, :, x, yl]
         for j, device in enumerate(peers):
             send(spectra.at[device["freq"], c], mine, a2a_send.at[c, j], a2a_recv.at[c], device)
         pltpu.make_async_copy(spectra.at[f, c], mine, a2a_recv.at[c]).start()
+        if c not in Z_FIRST:
+            for j, device in enumerate(beyond):
+                send(spectra.at[device["freq"], c], mine, b_send.at[c, j], y_recv.at[c, 0], device)
+
+    def pass_across(c, slot, dz):
+        block = held.at[c, owner(dz, 0)]
+        send(block, block, y_send.at[c, slot], y_recv.at[c, slot], across)
 
     def stage_own(c):
-        block = held.at[c, t]
-        arrived(block, a2a_recv.at[c])
-        send(block, block, y_send.at[c], y_recv.at[c], across)
+        arrived(held.at[c, t], a2a_recv.at[c])
+        if c not in Z_FIRST:
+            block = held.at[c, t, :, :, yl]
+            send(block, block, y_send.at[c, 0], y_recv.at[c, 0], across)
         whole_up_down(c, 0)
         share(c, 0, 0, 0)
 
-    def stage_across(c):
-        arrived(held.at[c, owner(0, 1)], y_recv.at[c])
-        whole_up_down(c, 1)
-        share(c, 1, 0, 1)
-
-    def stage_forward(c, plane):
+    def stage_near(c, plane=0):
         forward(c, plane)
         share(c, 2 + plane, 3, plane)
         share(c, 4 + plane, 1, plane)
 
+    def stage_fan(c):
+        for slot, dz in ((0, 0), (1, 3), (2, 1)):
+            pass_across(c, slot, dz)
+
     def stage_far(c):
-        for plane in range(2):
+        for plane in range(1 if c in Z_FIRST else 2):
             far = held.at[c, owner(2, plane)]
             arrived(far.at[0], f_recv.at[c, plane, 0])
             arrived(far.at[1], f_recv.at[c, plane, 1])
+            if c in Z_FIRST:
+                pass_across(c, 3, 2)
             share(c, 6 + plane, 2, plane)
+
+    def stage_across(c):
+        arrived(held.at[c, owner(0, 1)], y_recv.at[c, 0])
+        if c not in Z_FIRST:
+            whole_up_down(c, 1)
+        share(c, 1, 0, 1)
+        if c in Z_FIRST:
+            for slot, dz in ((1, 3), (2, 1), (3, 2)):
+                arrived(held.at[c, owner(dz, 1)], y_recv.at[c, slot])
+                share(c, 1 + 2 * slot, dz, 1)
 
     def stage_correlate(c):
         for slot, (dz, plane) in enumerate([(0, 0), (0, 1), (3, 0), (3, 1), (1, 0), (1, 1), (2, 0), (2, 1)]):
@@ -215,18 +239,21 @@
 
         lax.fori_loop(0, TM, column_block, 0)
 
-    stages = [
-        (0, stage_own),
-        (1, stage_across),
-        (1, functools.partial(stage_forward, plane=0)),
-        (2, functools.partial(stage_forward, plane=1)),
-        (3, stage_far),
-        (4, stage_correlate),
-    ]
-    for step in range(CH_DEV + 4):
-        for lag, stage in stages:
-            if 0 <= step - lag < CH_DEV:
-                stage(step - lag)
+    stages = {
+        "own": stage_own,
+        "near": stage_near,
+        "across": stage_across,
+        "near_across": functools.partial(stage_near, plane=1),
+        "fan": stage_fan,
+        "far": stage_far,
+        "correlate": stage_correlate,
+    }
+    events = []
+    for c in range(CH_DEV):
+        for name, time in (Z_TIMES if c in Z_FIRST else Y_TIMES).items():
+            events.append((c * (OWN_PACE if name == "own" else 1.0) + time, name, c))
+    for _, name, c in sorted(events, key=lambda event: event[0]):
+        stages[name](c)
     for src, sem in started:
         arrived(src, sem)
 
@@ -239,11 +266,12 @@
         in_specs=[pl.BlockSpec(memory_space=pltpu.VMEM)],
         out_specs=pl.BlockSpec(memory_space=pltpu.VMEM),
         scratch_shapes=[
-            pltpu.VMEM((CH_DEV, TM, 2, ROWS, S), jnp.bfloat16),
+            pltpu.VMEM((CH_DEV, TM, 2, 4, 2, A_DEV, S), jnp.bfloat16),
             dma((CH_DEV, FREQ - 1)),
             dma((CH_DEV,)),
-            dma((CH_DEV,)),
-            dma((CH_DEV,)),
+            dma((CH_DEV, 4)),
+            dma((CH_DEV, 4)),
+            dma((CH_DEV, 4)),
             dma((CH_DEV, 2, 2)),
             dma((CH_DEV, 2, 2)),
             dma((CH_DEV, 2, 2)),
@@ -258,9 +286,33 @@
     )(spectra)
 
 
+def write_kernel(block, out_ref, sem):
+    copies = [
+        pltpu.make_async_copy(block.at[q, c], out_ref.at[q, c], sem.at[q, c])
+        for q in range(2)
+        for c in range(CH_DEV)
+    ]
+    for copy in copies:
+        copy.start()
+    for copy in copies:
+        copy.wait()
+
+
+def write(block):
+    return pl.pallas_call(
+        write_kernel,
+        out_shape=jax.ShapeDtypeStruct(block.shape, block.dtype),
+        in_specs=[pl.BlockSpec(memory_space=pltpu.VMEM)],
+        out_specs=pl.BlockSpec(memory_space=pl.ANY),
+        scratch_shapes=[pltpu.SemaphoreType.DMA((2, CH_DEV))],
+        compiler_params=pltpu.CompilerParams(vmem_limit_bytes=20 * MIB),
+        name="write_coherence",
+    )(block)
+
+
 def on_device(voltages, fir_taps):
     spectra = channelize(voltages, fir_taps)
-    return correlate(spectra.reshape(FREQ, CH_DEV, 2, A_DEV, S))
+    return write(correlate(spectra.reshape(FREQ, CH_DEV, 2, A_DEV, S)))
 
 
 def solution(mesh):

time: 144 us -> 119 us (0.83)
  Pallas kernels: 130 us -> 118 us
  local copies, waits for them, and re-layouts: 12.9 us -> 1.22 us
    pallas_call x1, Pallas kernels: 101 us -> 85 us  [correlate(): pl.pallas_call(correlate_kernel, out_shape=jax.ShapeDtypeStruct((2, CH_DE...]
    unnamed x5 -> x2, local copies, waits for them, and re-layouts: 12.9 us -> 1.22 us
    pallas_call x0 -> x1, Pallas kernels: none -> 3.42 us  [write(): pl.pallas_call(write_kernel, out_shape=jax.ShapeDtypeStruct(block.shape,...]
where the time goes in v2:
time: 119 us
  Pallas kernels  118 us (99%)
  local copies, waits for them, and re-layouts  1.22 us (1%)
    pallas_call x1, Pallas kernels, correlate(): pl.pallas_call(correlate_kernel, out_shape=jax.ShapeDtypeStruct((2, CH_DE...  85 us
    pallas_call x1, Pallas kernels, channelize(): pl.pallas_call(channelize_kernel, out_shape=jax.ShapeDtypeStruct((rows, S...  29.5 us
    pallas_call x1, Pallas kernels, write(): pl.pallas_call(write_kernel, out_shape=jax.ShapeDtypeStruct(block.shape,...  3.42 us

profile of v2, /device:TPU:0, one launch (start us, length us, event | category | flops | bytes accessed | tf_op | source)
XLA Modules:
  0.0 119.2 jit_solution(5168010483615934316)
XLA Ops:
  0.0 29.5 %channelize.1 = bf16[2048,256]{1,0:T(8,128)(2,1)} custom-call(bf16[16,530432]{1,0:T(8,128)(2,1)} %v_hbm.1, f32[4,2048]{1,0:T(4,128)} %taps_ref.1, bf16[2048,128]{1,0:T(8,128)(2,1)} %constant.2.clone.table_ref), custom_call_target="tpu_custom_call" | custom-call | tf_op jit(solution)/shard_map/channelize/pallas_call | solution.py:96
  29.5 0.0 copy-start
  29.5 1.2 %copy-done = bf16[2048,256]{1,0:T(8,128)(2,1)S(1)} copy-done((bf16[2048,256]{1,0:T(8,128)(2,1)S(1)}, bf16[2048,256]{1,0:T(8,128)(2,1)}, u32[]{:S(2)}) %copy-start) | copy-done | bytes 1048600
  30.7 85.0 %gather_correlate.1.block = bf16[2,8,128,2048]{3,2,1,0:T(8,128)(2,1)S(1)} custom-call(bf16[8,8,2,16,256]{4,3,2,1,0:T(8,128)(2,1)S(1)} %bitcast.1), custom_call_target="tpu_custom_call" | custom-call | tf_op jit(solution)/shard_map/gather_correlate/pallas_call | solution.py:263
  115.8 3.4 %write_coherence.1 = bf16[2,8,128,2048]{3,2,1,0:T(8,128)(2,1)} custom-call(bf16[2,8,128,2048]{3,2,1,0:T(8,128)(2,1)S(1)} %gather_correlate.1.block), custom_call_target="tpu_custom_call" | custom-call | tf_op jit(solution)/shard_map/write_coherence/pallas_call | solution.py:302
Async XLA Ops:
  29.5 1.2 %copy-start = (bf16[2048,256]{1,0:T(8,128)(2,1)S(1)}, bf16[2048,256]{1,0:T(8,128)(2,1)}, u32[]{:S(2)}) copy-start(bf16[2048,256]{1,0:T(8,128)(2,1)} %channelize.1) | copy-start | bytes 3145732

commit v3 on v2

v3 whole, which is shorter than its diff:
```python
import functools

import jax
import jax.numpy as jnp
import ml_dtypes
import numpy as np
from jax import lax
from jax.experimental import pallas as pl
from jax.experimental.pallas import tpu as pltpu
from jax.sharding import PartitionSpec as P

P_SIZE = 2048
TAPS = 4
FIRST_BIN = 512
CH_DEV = 8
S = 256
A_DEV = 16
CHANNELS = 64
S_BLOCK = 32
COLUMNS = 256
TURNS = 4
ROWS = 128
TM = 16
FREQ = 8
MESH = pl.DeviceIdType.MESH
MIB = 1 << 20
CHUNKS = 8
PAIRS = CHUNKS // 2
Z_FIRST = (0, 2, 4)
Y_TIMES = {"own": 0.0, "near": 2.0, "across": 2.0, "near_across": 4.0, "far": 5.5}
Z_TIMES = {"own": 0.0, "near": 1.5, "fan": 1.5, "far": 3.0, "across": 6.0}
OWN_TIMES = (0.0, 1.0, 2.0, 2.5, 4.0, 4.5, 5.0, 5.5)
FILTER_TIMES = (-0.5, 0.5, 1.4, 2.3)
SECOND_TIME = 2.6
POWER_TIME, POWER_SEND_TIME = 6.2, 6.6
CORRELATE_TIMES = (11.5, 12.0, 13.0, 14.0)


def dft_table():
    points = np.arange(P_SIZE, dtype=np.int64)
    bins = FIRST_BIN + np.arange(CHANNELS, dtype=np.int64)
    angle = 2.0 * np.pi / P_SIZE * (points[:, None] * bins[None, :] % P_SIZE)
    table = np.concatenate([np.cos(angle), -np.sin(angle)], axis=1)
    return table.astype(ml_dtypes.bfloat16)


def kernel(
    v_hbm, taps_ref, table_ref, out_ref, v, even, odd, raw, turned, spectra, held, scales, row_scales,
    load_sem, a2a_send, a2a_recv, b_send, y_send, y_recv, z_send, z_recv, f_send, f_recv, c_send, c_recv, p_send, p_recv
):
    blocks = S // S_BLOCK
    per_half = blocks // 2
    per_block = P_SIZE // COLUMNS
    block_rows = S_BLOCK * A_DEV

    def load(i):
        low = 0 if i == 0 else (i * S_BLOCK + TAPS - 1) * P_SIZE
        high = ((i + 1) * S_BLOCK + TAPS - 1) * P_SIZE
        return pltpu.make_async_copy(v_hbm.at[:, low:high], v.at[:, low:high], load_sem.at[i])

    for i in range(blocks):
        load(i).start()

    f = lax.axis_index("freq")
    t = lax.axis_index("tm")
    z, yh, core = t // 4, t // 2 % 2, t % 2

    def owner(dz, other_y, other_core=0):
        return (z + dz) % 4 * 4 + (yh + other_y) % 2 * 2 + (core + other_core) % 2

    def there(dz, other_y, other_core=0):
        return {"freq": f, "tm": owner(dz, other_y, other_core)}

    up, down, across, sibling = there(1, 0), there(3, 0), there(0, 1), there(0, 0, 1)
    x, yl = f // 2, f % 2
    peers = [{"freq": (f + j) % FREQ, "tm": t} for j in range(1, FREQ)]
    beyond = [{"freq": (x + j) % 4 * 2 + 1 - yl, "tm": owner(0, 1)} for j in range(4)]

    barrier = pltpu.get_barrier_semaphore()
    column = [{"freq": f, "tm": (t + j) % TM} for j in range(1, TM)]
    greeted = [*peers, *beyond, *column]
    for device in greeted:
        pl.semaphore_signal(barrier, inc=1, device_id=device, device_id_type=MESH)

    def greet():
        pl.semaphore_wait(barrier, len(greeted))

    started = []

    def send(src, dst, send_sem, recv_sem, device):
        copy = pltpu.make_async_remote_copy(
            src_ref=src,
            dst_ref=dst,
            send_sem=send_sem,
            recv_sem=recv_sem,
            device_id=device,
            device_id_type=MESH,
        )
        copy.start()
        started.append((src, send_sem))

    def arrived(ref, sem):
        pltpu.make_async_copy(ref, ref, sem).wait()

    def share(c, slot, dz, other_y):
        block = held.at[c, owner(dz, other_y)]
        send(block, block, c_send.at[c, slot], c_recv.at[c, slot], sibling)

    def whole_up_down(c, plane):
        block = held.at[c, owner(0, plane)]
        send(block, block, z_send.at[c, plane, 0], z_recv.at[c, plane, 0], up)
        send(block, block, z_send.at[c, plane, 1], z_recv.at[c, plane, 1], down)

    def forward(c, plane):
        low, high = held.at[c, owner(3, plane)], held.at[c, owner(1, plane)]
        arrived(low, z_recv.at[c, plane, 0])
        send(low.at[0], low.at[0], f_send.at[c, plane, 0], f_recv.at[c, plane, 0], up)
        arrived(high, z_recv.at[c, plane, 1])
        send(high.at[1], high.at[1], f_send.at[c, plane, 1], f_recv.at[c, plane, 1], down)

    def filter_columns(frames, block, part):
        for chunk in range(COLUMNS // 128):
            column = pl.multiple_of(part * COLUMNS + chunk * 128, 128)
            base = pl.multiple_of(block * (S_BLOCK * P_SIZE) + column, 128)
            taps = [
                jnp.broadcast_to(taps_ref[k : k + 1, pl.ds(column, 128)], (A_DEV, 128))
                for k in range(TAPS)
            ]

            def sample(s):
                return v[:, pl.ds(base + s * P_SIZE, 128)].astype(jnp.float32)

            window = [sample(k) for k in range(TAPS - 1)]
            for s in range(S_BLOCK):
                window.append(sample(s + TAPS - 1))
                total = taps[0] * window[0]
                for k in range(1, TAPS):
                    total = total + taps[k] * window[k]
                frames[s * A_DEV : (s + 1) * A_DEV, chunk * 128 : (chunk + 1) * 128] = total.astype(jnp.bfloat16)
                window = window[1:]

    def transform(frames, block, part):
        rows = pl.ds(pl.multiple_of(block % per_half * block_rows, block_rows), block_rows)
        points = pl.ds(pl.multiple_of(part * COLUMNS, COLUMNS), COLUMNS)
        raw[rows, :] += jnp.dot(frames[...], table_ref[points, :], preferred_element_type=jnp.float32)

    def filter_block(i):
        load(i).wait()
        rows = slice(i % per_half * block_rows, (i % per_half + 1) * block_rows)
        raw[rows, :] = jnp.zeros((block_rows, 2 * CHANNELS), jnp.float32)
        if i % per_half == 0:
            odd[...] = jnp.zeros_like(odd)

        def pair(j, _):
            before = jnp.maximum(i * per_block + 2 * j - 1, i // per_half * per_half * per_block)
            filter_columns(even, i, 2 * j)
            transform(odd, before // per_block, before % per_block)
            filter_columns(odd, i, 2 * j + 1)
            transform(even, i, 2 * j)
            return 0

        lax.fori_loop(0, per_block // 2, pair, 0)

    def turn_half(h):
        transform(odd, (h + 1) * per_half - 1, per_block - 1)

        def turn(group, _):
            for k in range(TURNS):
                a = group * TURNS + k
                turned[pl.ds(a, 2 * CHANNELS, A_DEV), :] = raw[pl.ds(a, S // 2, A_DEV), :].T
            return 0

        lax.fori_loop(0, A_DEV // TURNS, turn, 0)

        def narrow(owner_freq, _):
            for pair in range(PAIRS):
                for k in range(2):
                    for r in range(2):
                        q = (r * CHANNELS + owner_freq * CH_DEV + pair * 2 + k) * A_DEV
                        rows = turned[pl.ds(pl.multiple_of(q, A_DEV), A_DEV), :]
                        spectra[h * PAIRS + pair, owner_freq, k, r] = rows.astype(jnp.bfloat16)
            return 0

        lax.fori_loop(0, FREQ, narrow, 0)

    def stage_exchange(h):
        for c in range(h * PAIRS, (h + 1) * PAIRS):
            mine = held.at[c, t, :, :, x, yl]
            for j, device in enumerate(peers):
                send(spectra.at[c, device["freq"]], mine, a2a_send.at[c, j], a2a_recv.at[c], device)
            pltpu.make_async_copy(spectra.at[c, f], mine, a2a_recv.at[c]).start()
            if c not in Z_FIRST:
                for j, device in enumerate(beyond):
                    send(spectra.at[c, device["freq"]], mine, b_send.at[c, j], y_recv.at[c, 0], device)

    def pass_across(c, slot, dz):
        block = held.at[c, owner(dz, 0)]
        send(block, block, y_send.at[c, slot], y_recv.at[c, slot], across)

    def stage_own(c):
        arrived(held.at[c, t], a2a_recv.at[c])
        if c not in Z_FIRST:
            block = held.at[c, t, :, :, :, yl]
            send(block, block, y_send.at[c, 0], y_recv.at[c, 0], across)
        whole_up_down(c, 0)
        share(c, 0, 0, 0)

    def stage_near(c, plane=0):
        forward(c, plane)
        share(c, 2 + plane, 3, plane)
        share(c, 4 + plane, 1, plane)

    def stage_fan(c):
        for slot, dz in ((0, 0), (1, 3), (2, 1)):
            pass_across(c, slot, dz)

    def stage_far(c):
        for plane in range(1 if c in Z_FIRST else 2):
            far = held.at[c, owner(2, plane)]
            arrived(far.at[0], f_recv.at[c, plane, 0])
            arrived(far.at[1], f_recv.at[c, plane, 1])
            if c in Z_FIRST:
                pass_across(c, 3, 2)
            share(c, 6 + plane, 2, plane)

    def stage_across(c):
        arrived(held.at[c, owner(0, 1)], y_recv.at[c, 0])
        if c not in Z_FIRST:
            whole_up_down(c, 1)
        share(c, 1, 0, 1)
        if c in Z_FIRST:
            for slot, dz in ((1, 3), (2, 1), (3, 2)):
                arrived(held.at[c, owner(dz, 1)], y_recv.at[c, slot])
                share(c, 1 + 2 * slot, dz, 1)

    def stage_power(_):
        for c in range(CH_DEV):
            total = jnp.zeros((ROWS, 1), jnp.float32)
            for h in range(2):
                for r in range(2):
                    part = held[h * PAIRS + c // 2, t, c % 2, r].reshape(ROWS, S // 2).astype(jnp.float32)
                    total = total + jnp.sum(part * part, axis=1, keepdims=True)
            scale = lax.rsqrt(total / S + 1e-6) * (1.0 / 16.0)
            scale = jnp.broadcast_to(scale, (ROWS, ROWS))
            row_scales[c] = scale
            scales[t, c : c + 1, :] = scale.T[0:1, :]

    def stage_power_send(_):
        for j in range(1, TM):
            block = scales.at[t]
            send(block, block, p_send.at[j - 1], p_recv.at[j - 1], {"freq": f, "tm": (t + j) % TM})

    def stage_correlate(pair):
        if pair == 0:
            for j in range(1, TM):
                arrived(scales.at[(t + TM - j) % TM], p_recv.at[j - 1])
        for c in (pair, PAIRS + pair):
            for slot, (dz, plane) in enumerate([(0, 0), (0, 1), (3, 0), (3, 1), (1, 0), (1, 1), (2, 0), (2, 1)]):
                arrived(held.at[c, owner(dz, plane, 1)], c_recv.at[c, slot])

        def both(b, k):
            halves = [held[h * PAIRS + pair, b, k].reshape(2 * ROWS, S // 2) for h in range(2)]
            return jnp.concatenate(halves, axis=1)

        for k in range(2):
            rows = both(t, k)
            c = pair * 2 + k

            def column_block(b, _, k=k, c=c, rows=rows):
                products = lax.dot_general(
                    rows, both(b, k), (((1,), (1,)), ((), ())), preferred_element_type=jnp.float32
                )
                lanes = pl.ds(pl.multiple_of(b * ROWS, ROWS), ROWS)
                scale = row_scales[c] * scales[b, c : c + 1, :]
                re = products[:ROWS, :ROWS] + products[ROWS:, ROWS:]
                im = products[ROWS:, :ROWS] - products[:ROWS, ROWS:]
                out_ref[0, c, :, lanes] = (re * scale).astype(jnp.bfloat16)
                out_ref[1, c, :, lanes] = (im * scale).astype(jnp.bfloat16)
                return 0

            lax.fori_loop(0, TM, column_block, 0)

    def stage_second(_):
        turn_half(1)
        stage_exchange(1)

    for i in range(per_half):
        filter_block(i)
    turn_half(0)
    greet()
    stage_exchange(0)

    stages = {
        "own": stage_own,
        "near": stage_near,
        "across": stage_across,
        "near_across": functools.partial(stage_near, plane=1),
        "fan": stage_fan,
        "far": stage_far,
        "filter": filter_block,
        "second": stage_second,
        "power": stage_power,
        "power_send": stage_power_send,
        "correlate": stage_correlate,
    }
    events = [(SECOND_TIME, "second", 0), (POWER_TIME, "power", 0), (POWER_SEND_TIME, "power_send", 0)]
    events += [(time, "filter", per_half + i) for i, time in enumerate(FILTER_TIMES)]
    events += [(time, "correlate", pair) for pair, time in enumerate(CORRELATE_TIMES)]
    for c in range(CHUNKS):
        for name, time in (Z_TIMES if c in Z_FIRST else Y_TIMES).items():
            events.append((OWN_TIMES[c] if name == "own" else c + time, name, c))
    for _, name, c in sorted(events, key=lambda event: event[0]):
        stages[name](c)
    for src, sem in started:
        arrived(src, sem)


def correlate(voltages, fir_taps):
    dma = pltpu.SemaphoreType.DMA
    vmem = pltpu.VMEM
    return pl.pallas_call(
        kernel,
        out_shape=jax.ShapeDtypeStruct((2, CH_DEV, ROWS, TM * ROWS), jnp.bfloat16),
        in_specs=[
            pl.BlockSpec(memory_space=pl.ANY),
            pl.BlockSpec(memory_space=vmem),
            pl.BlockSpec(memory_space=vmem),
        ],
        out_specs=pl.BlockSpec(memory_space=vmem),
        scratch_shapes=[
            vmem((A_DEV, (S + TAPS - 1) * P_SIZE), jnp.bfloat16),
            vmem((S_BLOCK * A_DEV, COLUMNS), jnp.bfloat16),
            vmem((S_BLOCK * A_DEV, COLUMNS), jnp.bfloat16),
            vmem((S // 2 * A_DEV, 2 * CHANNELS), jnp.float32),
            vmem((2 * CHANNELS * A_DEV, S // 2), jnp.float32),
            vmem((CHUNKS, FREQ, 2, 2, A_DEV, S // 2), jnp.bfloat16),
            vmem((CHUNKS, TM, 2, 2, 4, 2, A_DEV, S // 2), jnp.bfloat16),
            vmem((TM, CH_DEV, ROWS), jnp.float32),
            vmem((CH_DEV, ROWS, ROWS), jnp.float32),
            dma((S // S_BLOCK,)),
            dma((CHUNKS, FREQ - 1)),
            dma((CHUNKS,)),
            dma((CHUNKS, 4)),
            dma((CHUNKS, 4)),
            dma((CHUNKS, 4)),
            dma((CHUNKS, 2, 2)),
            dma((CHUNKS, 2, 2)),
            dma((CHUNKS, 2, 2)),
            dma((CHUNKS, 2, 2)),
            dma((CHUNKS, 8)),
            dma((CHUNKS, 8)),
            dma((TM - 1,)),
            dma((TM - 1,)),
        ],
        compiler_params=pltpu.CompilerParams(
            collective_id=0, has_side_effects=True, vmem_limit_bytes=42 * MIB
        ),
        name="channelize_gather_correlate",
    )(voltages, fir_taps, jnp.asarray(dft_table()))


def write_kernel(block, out_ref, sem):
    copies = [
        pltpu.make_async_copy(block.at[q, c], out_ref.at[q, c], sem.at[q, c])
        for q in range(2)
        for c in range(CH_DEV)
    ]
    for copy in copies:
        copy.start()
    for copy in copies:
        copy.wait()


def write(block):
    return pl.pallas_call(
        write_kernel,
        out_shape=jax.ShapeDtypeStruct(block.shape, block.dtype),
        in_specs=[pl.BlockSpec(memory_space=pltpu.VMEM)],
        out_specs=pl.BlockSpec(memory_space=pl.ANY),
        scratch_shapes=[pltpu.SemaphoreType.DMA((2, CH_DEV))],
        compiler_params=pltpu.CompilerParams(vmem_limit_bytes=20 * MIB),
        name="write_coherence",
    )(block)


def on_device(voltages, fir_taps):
    return write(correlate(voltages, fir_taps))


def solution(mesh):
    placed = (P(("tm", "freq"), None), P())
    return jax.shard_map(
        on_device,
        mesh=mesh,
        in_specs=placed,
        out_specs=P(None, "freq", "tm", None),
        check_vma=False,
    )
```

time: 119 us -> 116 us (0.975)
  Pallas kernels: 118 us -> 114 us
    pallas_call x2 -> x1, Pallas kernels: 115 us -> 111 us  [correlate(): pl.pallas_call(kernel, out_shape=jax.ShapeDtypeStruct((2, CH_DEV, ROWS, T...]
where the time goes in v3:
time: 116 us
  Pallas kernels  114 us (98%)
  local copies, waits for them, and re-layouts  1.8 us (2%)
    pallas_call x1, Pallas kernels, correlate(): pl.pallas_call(kernel, out_shape=jax.ShapeDtypeStruct((2, CH_DEV, ROWS, T...  111 us
    pallas_call x1, Pallas kernels, write(): pl.pallas_call(write_kernel, out_shape=jax.ShapeDtypeStruct(block.shape,...  3.42 us

profile of v3, /device:TPU:0, one launch (start us, length us, event | category | flops | bytes accessed | tf_op | source)
XLA Modules:
  0.0 116.0 jit_solution(878011661284794041)
XLA Ops:
  0.0 0.0 copy-start
  0.0 1.0 copy-done
  1.0 0.0 copy-start.1
  1.0 0.8 copy-done.1
  1.8 110.8 %channelize_gather_correlate.1.block = bf16[2,8,128,2048]{3,2,1,0:T(8,128)(2,1)S(1)} custom-call(bf16[16,530432]{1,0:T(8,128)(2,1)} %v_hbm.1, f32[4,2048]{1,0:T(4,128)S(1)} %copy-done.1, bf16[2048,128]{1,0:T(8,128)(2,1)S(1)} %copy-done), custom_call_target="tpu_custom_call" | custom-call | tf_op jit(solution)/shard_map/channelize_gather_correlate/pallas_call | solution.py:321
  112.6 3.4 %write_coherence.1 = bf16[2,8,128,2048]{3,2,1,0:T(8,128)(2,1)} custom-call(bf16[2,8,128,2048]{3,2,1,0:T(8,128)(2,1)S(1)} %channelize_gather_correlate.1.block), custom_call_target="tpu_custom_call" | custom-call | tf_op jit(solution)/shard_map/write_coherence/pallas_call | solution.py:375
Async XLA Ops:
  0.0 1.0 copy-start
  1.0 0.8 copy-start.1

commit v4 on v3

--- a/solution.py
+++ b/solution.py
@@ -26,14 +26,20 @@
 MIB = 1 << 20
 CHUNKS = 8
 PAIRS = CHUNKS // 2
-Z_FIRST = (0, 2, 4)
-Y_TIMES = {"own": 0.0, "near": 2.0, "across": 2.0, "near_across": 4.0, "far": 5.5}
-Z_TIMES = {"own": 0.0, "near": 1.5, "fan": 1.5, "far": 3.0, "across": 6.0}
-OWN_TIMES = (0.0, 1.0, 2.0, 2.5, 4.0, 4.5, 5.0, 5.5)
-FILTER_TIMES = (-0.5, 0.5, 1.4, 2.3)
-SECOND_TIME = 2.6
-POWER_TIME, POWER_SEND_TIME = 6.2, 6.6
-CORRELATE_TIMES = (11.5, 12.0, 13.0, 14.0)
+Z_FIRST = (1, 3, 4)
+ORDER = (
+    ("filter", 4), ("filter", 5), ("own", 0), ("filter", 6), ("own", 1), ("filter", 7), ("own", 2),
+    ("second", 0), ("near", 0), ("across", 0), ("near", 1), ("fan", 1), ("near", 2), ("own", 4),
+    ("near_across", 0), ("own", 5), ("far", 1), ("own", 3), ("near", 4), ("own", 6), ("fan", 4), ("near", 5),
+    ("far", 0), ("across", 5), ("far", 4), ("own", 7), ("across", 1), ("across", 2), ("power", 0),
+    ("near_across", 5), ("across", 6), ("near", 3), ("fan", 3), ("near", 6), ("power_send", 0),
+    ("near_across", 2), ("far", 5), ("across", 4), ("near_across", 6), ("across", 7), ("near", 7), ("far", 3),
+    ("correlate", 2), ("correlate", 3), ("far", 2), ("far", 6), ("correlate", 0), ("near_across", 7),
+    ("correlate", 1), ("across", 3), ("correlate", 4), ("far", 7), ("correlate", 5), ("correlate", 6),
+    ("correlate", 7),
+)
+WIDE = 4
+FIRST_CHANNEL = 2
 
 
 def dft_table():
@@ -250,35 +256,39 @@
             block = scales.at[t]
             send(block, block, p_send.at[j - 1], p_recv.at[j - 1], {"freq": f, "tm": (t + j) % TM})
 
-    def stage_correlate(pair):
-        if pair == 0:
+    def stage_correlate(c):
+        pair, k = c // 2, c % 2
+        if c == FIRST_CHANNEL:
             for j in range(1, TM):
                 arrived(scales.at[(t + TM - j) % TM], p_recv.at[j - 1])
-        for c in (pair, PAIRS + pair):
-            for slot, (dz, plane) in enumerate([(0, 0), (0, 1), (3, 0), (3, 1), (1, 0), (1, 1), (2, 0), (2, 1)]):
-                arrived(held.at[c, owner(dz, plane, 1)], c_recv.at[c, slot])
-
-        def both(b, k):
+        if k == 0:
+            for chunk in (pair, PAIRS + pair):
+                for slot, (dz, plane) in enumerate([(0, 0), (0, 1), (3, 0), (3, 1), (1, 0), (1, 1), (2, 0), (2, 1)]):
+                    arrived(held.at[chunk, owner(dz, plane, 1)], c_recv.at[chunk, slot])
+
+        def both(b):
             halves = [held[h * PAIRS + pair, b, k].reshape(2 * ROWS, S // 2) for h in range(2)]
             return jnp.concatenate(halves, axis=1)
 
-        for k in range(2):
-            rows = both(t, k)
-            c = pair * 2 + k
-
-            def column_block(b, _, k=k, c=c, rows=rows):
-                products = lax.dot_general(
-                    rows, both(b, k), (((1,), (1,)), ((), ())), preferred_element_type=jnp.float32
-                )
-                lanes = pl.ds(pl.multiple_of(b * ROWS, ROWS), ROWS)
-                scale = row_scales[c] * scales[b, c : c + 1, :]
-                re = products[:ROWS, :ROWS] + products[ROWS:, ROWS:]
-                im = products[ROWS:, :ROWS] - products[:ROWS, ROWS:]
+        rows = both(t)
+
+        def column_blocks(group, _):
+            first = group * WIDE
+            columns = jnp.concatenate([both(first + i) for i in range(WIDE)], axis=0)
+            products = lax.dot_general(
+                rows, columns, (((1,), (1,)), ((), ())), preferred_element_type=jnp.float32
+            )
+            for i in range(WIDE):
+                block = products[:, i * 2 * ROWS : (i + 1) * 2 * ROWS]
+                lanes = pl.ds(pl.multiple_of((first + i) * ROWS, ROWS), ROWS)
+                scale = row_scales[c] * scales[first + i, c : c + 1, :]
+                re = block[:ROWS, :ROWS] + block[ROWS:, ROWS:]
+                im = block[ROWS:, :ROWS] - block[:ROWS, ROWS:]
                 out_ref[0, c, :, lanes] = (re * scale).astype(jnp.bfloat16)
                 out_ref[1, c, :, lanes] = (im * scale).astype(jnp.bfloat16)
-                return 0
-
-            lax.fori_loop(0, TM, column_block, 0)
+            return 0
+
+        lax.fori_loop(0, TM // WIDE, column_blocks, 0)
 
     def stage_second(_):
         turn_half(1)
@@ -303,13 +313,7 @@
         "power_send": stage_power_send,
         "correlate": stage_correlate,
     }
-    events = [(SECOND_TIME, "second", 0), (POWER_TIME, "power", 0), (POWER_SEND_TIME, "power_send", 0)]
-    events += [(time, "filter", per_half + i) for i, time in enumerate(FILTER_TIMES)]
-    events += [(time, "correlate", pair) for pair, time in enumerate(CORRELATE_TIMES)]
-    for c in range(CHUNKS):
-        for name, time in (Z_TIMES if c in Z_FIRST else Y_TIMES).items():
-            events.append((OWN_TIMES[c] if name == "own" else c + time, name, c))
-    for _, name, c in sorted(events, key=lambda event: event[0]):
+    for name, c in ORDER:
         stages[name](c)
     for src, sem in started:
         arrived(src, sem)

time: 116 us -> 95.6 us (0.82)
  Pallas kernels: 114 us -> 92.8 us
    pallas_call x1, Pallas kernels: 111 us -> 89.4 us  [correlate(): pl.pallas_call(kernel, out_shape=jax.ShapeDtypeStruct((2, CH_DEV, ROWS, T...]
where the time goes in v4:
time: 95.6 us; the launch traced here: 94.6 us
  Pallas kernels  92.8 us (97%)
  local copies, waits for them, and re-layouts  1.8 us (2%)
    pallas_call x1, Pallas kernels, correlate(): pl.pallas_call(kernel, out_shape=jax.ShapeDtypeStruct((2, CH_DEV, ROWS, T...  89.4 us
    pallas_call x1, Pallas kernels, write(): pl.pallas_call(write_kernel, out_shape=jax.ShapeDtypeStruct(block.shape,...  3.42 us

profile of v4, /device:TPU:0, one launch (start us, length us, event | category | flops | bytes accessed | tf_op | source)
XLA Modules:
  0.0 94.6 jit_solution(14372979828752863398)
XLA Ops:
  0.0 0.0 copy-start
  0.0 1.0 %copy-done = bf16[2048,128]{1,0:T(8,128)(2,1)S(1)} copy-done((bf16[2048,128]{1,0:T(8,128)(2,1)S(1)}, bf16[2048,128]{1,0:T(8,128)(2,1)}, u32[]{:S(2)}) %copy-start) | copy-done | bytes 524312
  1.0 0.0 copy-start.1
  1.0 0.8 copy-done.1
  1.8 89.4 %channelize_gather_correlate.1.block = bf16[2,8,128,2048]{3,2,1,0:T(8,128)(2,1)S(1)} custom-call(bf16[16,530432]{1,0:T(8,128)(2,1)} %v_hbm.1, f32[4,2048]{1,0:T(4,128)S(1)} %copy-done.1, bf16[2048,128]{1,0:T(8,128)(2,1)S(1)} %copy-done), custom_call_target="tpu_custom_call" | custom-call | tf_op jit(solution)/shard_map/channelize_gather_correlate/pallas_call | solution.py:325
  91.2 3.4 %write_coherence.1 = bf16[2,8,128,2048]{3,2,1,0:T(8,128)(2,1)} custom-call(bf16[2,8,128,2048]{3,2,1,0:T(8,128)(2,1)S(1)} %channelize_gather_correlate.1.block), custom_call_target="tpu_custom_call" | custom-call | tf_op jit(solution)/shard_map/write_coherence/pallas_call | solution.py:379
Async XLA Ops:
  0.0 1.0 %copy-start = (bf16[2048,128]{1,0:T(8,128)(2,1)S(1)}, bf16[2048,128]{1,0:T(8,128)(2,1)}, u32[]{:S(2)}) copy-start(bf16[2048,128]{1,0:T(8,128)(2,1)} %constant.2.clone.table_ref) | copy-start | bytes 1572868
  1.0 0.8 copy-start.1
